TPU v7x, 1024 devices: a whole 4x8x16 slice. The times are simulated.
1024 devices in a mesh: section: 64 (over z, x), ctx: 16 (over y, core).
Axes of the slice: x: 4, y: 8, z: 16, core: 2. Of those that a mesh axis runs over, the one named last changes fastest.
Arguments:
- activations: bfloat16 [64, 24, 8192], P('section'), may hold values from -6 to 6
- act_frames: int32 [64, 24], replicated, may hold values from 0 to 191
- fresh_batch: bfloat16 [24, 8192], replicated, may hold values from -6 to 6
- fresh_frames: int32 [24], replicated, may hold values from 0 to 191
- norm_gain: float32 [64, 8192], P('section'), may hold values from 0.1 to 1.9
- cached_keys: bfloat16 [64, 12288, 1024], P('section', 'ctx'), may hold values from -64 to 64
- cached_values: bfloat16 [64, 12288, 1024], P('section', 'ctx'), may hold values from -6 to 6
- key_frames: int32 [12288], P('ctx'), may hold values from 0 to 191, never falling along the last dimension, each value on 1 to 128 neighbouring positions
Outputs:
- result: bfloat16 [64, 24, 8192], P('section')
Inputs may be any that keep to these rules, and one draw needn't show every extreme that they name: `key_frames`: frame indices never fall along the clip, and every frame of 0 to 191 holds at least one token.
All inputs are finite; a program needn't handle non-finite values.
Results may differ from a plain program's by a relative error of at most 0.019.
Values may be sent and summed in bfloat16 or wider, within the bound.
A program may use at most 64 MiB of HBM per device.

v0:
```python
import jax
import jax.numpy as jnp
from jax import lax
from jax.sharding import PartitionSpec as P

HEADS = 64
HD = 128


epsilon = 1e-05
masked_score = -1e30


def passed_along(block, axis, distance):
    devices = range(lax.axis_size(axis))
    route = [(i - distance, i) for i in devices if i - distance in devices]
    return lax.ppermute(block, axis, route)


def partial_terms(
    hidden, frames, norm_scale, key_cache, value_cache, key_frames, head_count, head_size
):
    token_count = hidden.shape[0]
    kv_heads = key_cache.shape[1] // head_size
    widened = hidden.astype(jnp.float32)
    per_head = widened.reshape(token_count, head_count, head_size)
    scale_heads = norm_scale.reshape(head_count, head_size)
    queries = (
        per_head
        * lax.rsqrt(jnp.mean(per_head * per_head, axis=-1, keepdims=True) + epsilon)
        * scale_heads[None]
    ).astype(jnp.bfloat16)
    grouped = queries.reshape(token_count, kv_heads, head_count // kv_heads, head_size)
    key_rows = key_cache.reshape(-1, kv_heads, head_size)
    value_rows = value_cache.reshape(-1, kv_heads, head_size)
    scores = jnp.einsum(
        "tkgd,jkd->tkgj", grouped, key_rows, preferred_element_type=jnp.float32
    ) * head_size ** (-0.5)
    visible = key_frames[None, None, None, :] <= frames[:, None, None, None]
    scores = jnp.where(visible, scores, masked_score)
    block_max = jnp.max(scores, axis=-1)
    probabilities = jnp.where(visible, jnp.exp(scores - block_max[..., None]), 0.0).astype(
        jnp.bfloat16
    )
    totals = jnp.sum(probabilities.astype(jnp.float32), axis=-1)
    weighted = jnp.einsum(
        "tkgj,jkd->tkgd", probabilities, value_rows, preferred_element_type=jnp.float32
    )
    partials = (
        block_max.reshape(token_count, head_count),
        totals.reshape(token_count, head_count),
        weighted.reshape(token_count, head_count, head_size),
    )
    return (widened, partials)


def layer(hidden, frames, norm_scale, key_cache, value_cache, key_frames):
    widened, partials = partial_terms(
        hidden, frames, norm_scale, key_cache, value_cache, key_frames, HEADS, HD
    )
    overall = lax.pmax(partials[0], "ctx")
    factors = jnp.exp(partials[0] - overall)
    denominator, numerator = lax.psum(
        (factors * partials[1], factors[..., None] * partials[2]), "ctx"
    )
    attended = (numerator / denominator[..., None]).reshape(widened.shape)
    return (widened + attended).astype(jnp.bfloat16)


def body(
    activations,
    act_frames,
    fresh_batch,
    fresh_frames,
    norm_gain,
    cached_keys,
    cached_values,
    key_frames,
):
    section_index = lax.axis_index("section")
    own_frames = lax.dynamic_index_in_dim(act_frames, section_index, 0, keepdims=False)
    first_out = layer(
        activations[0], own_frames, norm_gain[0], cached_keys[0], cached_values[0], key_frames
    )
    handed = passed_along(first_out, "section", 1)
    prior_frames = lax.dynamic_index_in_dim(
        act_frames, jnp.maximum(section_index - 1, 0), 0, keepdims=False
    )
    incoming = jnp.where(section_index == 0, fresh_batch, handed)
    frames_in = jnp.where(section_index == 0, fresh_frames, prior_frames)
    second = layer(incoming, frames_in, norm_gain[0], cached_keys[0], cached_values[0], key_frames)
    return second[None]


def solution(mesh):
    placed = (
        P("section", None, None),
        P(),
        P(),
        P(),
        P("section", None),
        P("section", "ctx", None),
        P("section", "ctx", None),
        P("ctx"),
    )
    return jax.shard_map(
        body, mesh=mesh, in_specs=placed, out_specs=P("section", None, None), check_vma=False
    )
```

profile of v0, /device:TPU:1, one launch (start us, length us, event | category | flops | bytes accessed | tf_op | source)
XLA Modules:
  0.0 415.1 jit_solution(4977624390474796012)
XLA Ops:
  6.5 0.0 all-reduce.3.cloned.1.call-start
  6.5 1.0 convert_bitcast_fusion
  7.6 1.1 fusion.24
  8.6 0.1 copy.63
  8.8 0.0 copy-start.5
  8.8 0.0 copy-start.7
  8.8 0.0 copy-start.6
  8.8 0.0 copy-start.4
  8.8 0.1 copy.64
  9.0 0.3 reduce_sum.36
  9.3 0.1 copy.31
  9.4 0.1 copy.32
  9.5 1.9 copy.65
  11.3 3.0 copy.66
  14.4 0.0 copy-done.5
  14.4 0.2 dynamic-slice_reduce_fusion
  14.5 0.0 copy-done.7
  14.6 0.0 copy-done.6
  14.6 0.1 broadcast_compare_fusion
  14.7 0.0 copy-done.4
  14.7 3.4 bitcast_reduce_fusion.1
  18.1 0.1 copy.35
  18.1 56.3 %pmax.14 = f32[24,64]{0,1:T(8,128)S(1)} all-reduce(f32[24,64]{0,1:T(8,128)S(1)} %bitcast.101), channel_id=1, replica_groups=mesh['section'=64,'ctx'=16] {'ctx'}, use_global_device_ids=true, to_apply=%region_2.3 | all-reduce | flops 1536 | bytes 12288 | tf_op jit(solution)/shard_map/pmax | solution.py:61
  74.5 4.2 %convert_reduce_fusion.1 = f32[24,8,8]{2,0,1:T(8,128)S(1)} fusion(f32[24,8,8]{2,0,1:T(8,128)S(1)} %get-tuple-element.15, f32[8,24,8,768]{3,2,1,0:T(8,128)} %get-tuple-element.16, pred[24,768]{1,0:T(8,128)(4,1)S(1)} %get-tuple-element.14), kind=kLoop, calls=%fused_computation.12 | loop fusion | flops 8256000 | bytes 4749312 | tf_op jit(solution)/shard_map/reduce_sum | solution.py:45
  78.7 0.0 copy-done
  78.7 0.0 copy-start.1
  78.7 3.0 fusion.14
  81.7 0.0 copy-start.3
  81.7 0.1 copy.39
  81.8 0.1 copy.36
  81.9 1.2 bitcast_multiply_fusion.1
  83.1 0.0 all-reduce.3.cloned.1.call-update
  83.1 0.0 all-reduce.5.cloned.1.call-start
  83.2 45.8 %psum.29 = f32[24,64]{0,1:T(8,128)S(1)} all-reduce(f32[24,64]{0,1:T(8,128)S(1)} %get-tuple-element.11), channel_id=1, replica_groups=mesh['section'=64,'ctx'=16] {'ctx'}, use_global_device_ids=true, to_apply=%region_5.6 | all-reduce | flops 1536 | bytes 12288 | tf_op jit(solution)/shard_map/psum | solution.py:63
  128.9 0.1 copy.40
  129.0 79.0 %all-reduce.3.cloned.1.call-done = f32[24,64,128]{2,1,0:T(8,128)} async-done(((f32[24,64,128]{2,1,0:T(8,128)}), f32[24,64,128]{2,1,0:T(8,128)}) %all-reduce.3.cloned.1.call-update) | async-done | bytes 786448 | tf_op jit(solution)/shard_map/psum | solution.py:63
  208.0 1.4 broadcast_divide_fusion.1
  209.4 0.0 copy-done.1
  209.4 0.5 fusion.23
  209.9 3.3 collective-permute-start
  213.2 7.4 %collective-permute-done = bf16[24,8192]{1,0:T(8,128)(2,1)S(1)} collective-permute-done((bf16[24,8192]{1,0:T(8,128)(2,1)S(1)}, bf16[24,8192]{1,0:T(8,128)(2,1)S(1)}, u32[]{:S(2)}, u32[]{:S(2)}) %collective-permute-start) | collective-permute-done | bytes 393248 | tf_op jit(solution)/shard_map/ppermute | solution.py:17
  220.6 0.0 copy-done.3
  220.6 0.1 fusion.20
  220.8 0.1 copy.69
  220.9 0.3 reduce_sum.38
  221.2 0.1 copy.41
  221.3 0.1 copy.42
  221.4 0.1 convert_bitcast_fusion.2
  221.4 0.0 copy-start.2
  221.4 0.1 copy.68
  221.6 1.4 bitcast_reduce_fusion
  223.0 1.5 fusion.17
  224.5 1.8 convert_reduce_fusion
  226.3 0.1 copy.45
  226.4 0.1 copy.49
  226.4 45.0 %pmax.15 = f32[24,64]{0,1:T(8,128)S(1)} all-reduce(f32[24,64]{0,1:T(8,128)S(1)} %bitcast.102), channel_id=1, replica_groups=mesh['section'=64,'ctx'=16] {'ctx'}, use_global_device_ids=true, to_apply=%region_8.9 | all-reduce | flops 1536 | bytes 12288 | tf_op jit(solution)/shard_map/pmax | solution.py:61
  271.4 0.1 copy.46
  271.5 1.2 bitcast_multiply_fusion
  272.7 0.0 all-reduce.5.cloned.1.call-update
  272.7 45.7 %psum.31 = f32[24,64]{0,1:T(8,128)S(1)} all-reduce(f32[24,64]{0,1:T(8,128)S(1)} %get-tuple-element.7), channel_id=1, replica_groups=mesh['section'=64,'ctx'=16] {'ctx'}, use_global_device_ids=true, to_apply=%region_11.12 | all-reduce | flops 1536 | bytes 12288 | tf_op jit(solution)/shard_map/psum | solution.py:63
  318.4 0.1 copy.50
  318.5 87.1 %all-reduce.5.cloned.1.call-done = f32[24,64,128]{2,1,0:T(8,128)} async-done(((f32[24,64,128]{2,1,0:T(8,128)}), f32[24,64,128]{2,1,0:T(8,128)}) %all-reduce.5.cloned.1.call-update) | async-done | bytes 786448 | tf_op jit(solution)/shard_map/psum | solution.py:63
  405.6 1.4 broadcast_divide_fusion
  407.0 1.2 fusion.31
  (7 shorter events, 0.1 us)
Async XLA Ops:
  6.5 201.5 %all-reduce.3.cloned.1.call-start = ((), (), s32[]{:S(2)}) async-start(), calls=%async_computation | async-start | bytes 1572864 | tf_op jit(solution)/shard_map/psum | solution.py:63
  8.8 5.6 %copy-start.5 = (s32[64,24]{0,1:T(8,128)S(1)}, s32[64,24]{0,1:T(8,128)}, u32[]{:S(2)}) copy-start(s32[64,24]{0,1:T(8,128)} %param.9) | copy-start | bytes 18436
  8.8 5.7 %copy-start.7 = (s32[24]{0:T(128)S(1)}, s32[24]{0:T(128)}, u32[]{:S(2)}) copy-start(s32[24]{0:T(128)} %param.11) | copy-start | bytes 292
  8.8 5.8 %copy-start.6 = (s32[768]{0:T(1024)S(1)}, s32[768]{0:T(1024)}, u32[]{:S(2)}) copy-start(s32[768]{0:T(1024)} %param.15) | copy-start | bytes 9220
  8.8 5.8 %copy-start.4 = (f32[1,8192]{1,0:T(1,128)S(1)}, f32[1,8192]{1,0:T(1,128)}, u32[]{:S(2)}) copy-start(f32[1,8192]{1,0:T(1,128)} %param.12) | copy-start | bytes 98308
  74.5 4.2 %copy-start = (f32[8,24,8,768]{3,2,1,0:T(8,128)S(1)}, f32[8,24,8,768]{3,2,1,0:T(8,128)}, u32[]{:S(2)}) copy-start(f32[8,24,8,768]{3,2,1,0:T(8,128)} %get-tuple-element.16) | copy-start | bytes 14155780
  78.7 130.7 %copy-start.1 = (bf16[1,24,8192]{2,1,0:T(8,128)(2,1)S(1)}, bf16[1,24,8192]{2,1,0:T(8,128)(2,1)}, u32[]{:S(2)}) copy-start(bf16[1,24,8192]{2,1,0:T(8,128)(2,1)} %param.8) | copy-start | bytes 1179652
  81.7 138.9 %copy-start.3 = (bf16[24,8192]{1,0:T(8,128)(2,1)S(1)}, bf16[24,8192]{1,0:T(8,128)(2,1)}, u32[]{:S(2)}) copy-start(bf16[24,8192]{1,0:T(8,128)(2,1)} %param.10) | copy-start | bytes 1179652
  83.1 322.5 %all-reduce.5.cloned.1.call-start = ((), (), s32[]{:S(2)}) async-start(), calls=%async_computation.1 | async-start | bytes 1572864 | tf_op jit(solution)/shard_map/psum | solution.py:63
  209.9 10.7 %collective-permute-start = (bf16[24,8192]{1,0:T(8,128)(2,1)S(1)}, bf16[24,8192]{1,0:T(8,128)(2,1)S(1)}, u32[]{:S(2)}, u32[]{:S(2)}) collective-permute-start(bf16[24,8192]{1,0:T(8,128)(2,1)S(1)} %fusion.23), channel_id=1, source_target_pairs={{0,16},{16,32},{32,48},{48,64},{64,80},{80,96},{96,112},{112,128},... | collective-permute-start | bytes 1179656 | tf_op jit(solution)/shard_map/ppermute | solution.py:17
  221.4 1.5 copy-start.2
Sparse Core Ops, SparseCore 0:
  83.2 124.7 all-reduce.2
  272.8 132.7 all-reduce.4
where the time goes:
time: 416 us; the launch traced here: 415 us
  blocking collectives  193 us (46%)
  waiting for transfers between devices  174 us (42%)
  other arithmetic  15.8 us (4%)
  between operations  13.7 us (3%)
  matrix products  9.26 us (2%)
  local copies, waits for them, and re-layouts  6.57 us (2%)
    psum x2, waiting for transfers between devices, layer(): lax.psum((factors * partials[1], factors[..., None] * partials[2]), 'ctx')  166 us
    pmax x2, blocking collectives, layer(): overall = lax.pmax(partials[0], 'ctx')  101 us
    psum x2, blocking collectives, layer(): lax.psum((factors * partials[1], factors[..., None] * partials[2]), 'ctx')  91.5 us
  transfers between devices with their start and end apart: 3, of which 3 were waited for; matrix products, arithmetic and copies ran while one was open for 0% of the time, Pallas kernels for 0%

commit v1 on v0

v1 whole, which is shorter than its diff:
```python
import functools
import math

import jax
import jax.numpy as jnp
from jax import lax
from jax.experimental import pallas as pl
from jax.experimental.pallas import tpu as pltpu
from jax.sharding import PartitionSpec as P

HD = 128
GROUP = 8
EPSILON = 1e-05
MASKED = -1e30
MESH = pl.DeviceIdType.MESH
EXPONENT_SCALE = HD**-0.5 * math.log2(math.e)


def kernel(
    n_sections,
    n_chips,
    act_hbm,
    act_frames_hbm,
    fresh_hbm,
    fresh_frames_hbm,
    gain_hbm,
    keys_hbm,
    values_hbm,
    key_frames_hbm,
    out_ref,
    act,
    fresh,
    act_frames,
    fresh_frames,
    gain,
    key_frames,
    keys,
    values,
    bias,
    scores,
    probs,
    sent,
    sent_stats,
    arrived,
    arrived_stats,
    combined,
    handed,
    local_sem,
    keys_sem,
    values_sem,
    pair_send_sem,
    pair_recv_sem,
    frames_send_sem,
    frames_recv_sem,
    part_send_sem,
    part_recv_sem,
    stat_send_sem,
    stat_recv_sem,
    hand_send_sem,
    hand_recv_sem,
    out_send_sem,
    out_recv_sem,
    cross_send_sem,
    cross_recv_sem,
):
    tokens = act.shape[0]
    own_keys = keys_hbm.shape[0]
    kv_heads = keys.shape[0]
    plane = act.shape[1]
    chunk_columns = plane // n_chips
    heads_in_chunk = chunk_columns // HD
    chunk_rows = heads_in_chunk * tokens
    chunks_per_head = GROUP * tokens // chunk_rows

    section = lax.axis_index("section")
    ctx = lax.axis_index("ctx")
    chip, core = ctx // 2, ctx % 2
    other = 1 - core
    following = (section + 1) % n_sections
    previous = (section + n_sections - 1) % n_sections
    sibling = (section, chip * 2 + other)

    def in_section(j):
        return (section, j * 2 + core)

    def columns(j, width):
        return pl.ds(pl.multiple_of(j * width, width), width)

    own_rows = pl.ds(pl.multiple_of(core * own_keys, own_keys), own_keys)
    locals_ = [
        pltpu.make_async_copy(act_hbm.at[:, columns(core, plane)], act, local_sem.at[0]),
        pltpu.make_async_copy(act_frames_hbm, act_frames, local_sem.at[1]),
        pltpu.make_async_copy(fresh_hbm.at[:, columns(core, plane)], fresh, local_sem.at[2]),
        pltpu.make_async_copy(fresh_frames_hbm, fresh_frames, local_sem.at[3]),
        pltpu.make_async_copy(gain_hbm.at[:, columns(core, plane)], gain, local_sem.at[4]),
        pltpu.make_async_copy(key_frames_hbm, key_frames.at[core], local_sem.at[5]),
    ]
    for copy in locals_:
        copy.start()

    def own_copies(h):
        return (
            pltpu.make_async_copy(
                keys_hbm.at[:, columns(core * kv_heads + h, HD)],
                keys.at[h, own_rows, :],
                keys_sem.at[h],
            ),
            pltpu.make_async_copy(
                values_hbm.at[:, columns(core * kv_heads + h, HD)],
                values.at[h, own_rows, pl.ds(0, HD)],
                values_sem.at[h],
            ),
        )

    def pair_copies(h):
        return (
            pltpu.make_async_remote_copy(
                src_ref=keys_hbm.at[:, columns(other * kv_heads + h, HD)],
                dst_ref=keys.at[h, own_rows, :],
                send_sem=pair_send_sem.at[h, 0],
                recv_sem=pair_recv_sem.at[h, 0],
                device_id=sibling,
                device_id_type=MESH,
            ),
            pltpu.make_async_remote_copy(
                src_ref=values_hbm.at[:, columns(other * kv_heads + h, HD)],
                dst_ref=values.at[h, own_rows, pl.ds(0, HD)],
                send_sem=pair_send_sem.at[h, 1],
                recv_sem=pair_recv_sem.at[h, 1],
                device_id=sibling,
                device_id_type=MESH,
            ),
        )

    other_rows = pl.ds(pl.multiple_of(other * own_keys, own_keys), own_keys)

    def pair_arrivals(h):
        return (
            pltpu.make_async_remote_copy(
                src_ref=keys.at[h, other_rows, :],
                dst_ref=keys.at[h, other_rows, :],
                send_sem=pair_send_sem.at[h, 0],
                recv_sem=pair_recv_sem.at[h, 0],
                device_id=sibling,
                device_id_type=MESH,
            ),
            pltpu.make_async_remote_copy(
                src_ref=values.at[h, other_rows, pl.ds(0, HD)],
                dst_ref=values.at[h, other_rows, pl.ds(0, HD)],
                send_sem=pair_send_sem.at[h, 1],
                recv_sem=pair_recv_sem.at[h, 1],
                device_id=sibling,
                device_id_type=MESH,
            ),
        )

    def visit(i):
        step = jnp.where(i == 0, 2, jnp.where(i == 1, 1, jnp.where(i == 2, 3, 0)))
        return (chip // chunks_per_head + step) % kv_heads

    for i in range(kv_heads):
        for copy in own_copies(visit(i)):
            copy.start()

    barrier = pltpu.get_barrier_semaphore()
    pl.semaphore_signal(barrier, inc=1, device_id=sibling, device_id_type=MESH)

    @pl.loop(0, n_chips)
    def _(j):
        @pl.when(j != chip)
        def _():
            pl.semaphore_signal(barrier, inc=1, device_id=in_section(j), device_id_type=MESH)

        for side in (previous, following):
            pl.semaphore_signal(
                barrier, inc=1, device_id=(side, j * 2 + core), device_id_type=MESH
            )

    pl.semaphore_wait(barrier, 1 + (n_chips - 1) + 2 * n_chips)

    frames_copy = pltpu.make_async_remote_copy(
        src_ref=key_frames_hbm,
        dst_ref=key_frames.at[core],
        send_sem=frames_send_sem,
        recv_sem=frames_recv_sem,
        device_id=sibling,
        device_id_type=MESH,
    )
    frames_copy.start()
    for i in range(kv_heads):
        for copy in pair_copies(visit(i)):
            copy.start()

    for h in range(kv_heads):
        values[h, :, HD:] = jnp.ones((values.shape[1], HD), values.dtype)
    for copy in locals_:
        copy.wait()
    frames_copy.wait()

    def set_bias(row):
        rows = lax.broadcasted_iota(jnp.int32, (tokens, tokens), 0)
        lanes = lax.broadcasted_iota(jnp.int32, (tokens, tokens), 1)
        spread = jnp.broadcast_to(row, (tokens, tokens)).astype(jnp.float32)
        column = jnp.sum(jnp.where(rows == lanes, spread, 0.0), axis=1, keepdims=True)
        for side in range(2):
            frames = key_frames[side].astype(jnp.float32)
            shown = jnp.where(frames <= column, 0.0, MASKED)
            bias[0:tokens, side * own_keys : (side + 1) * own_keys] = shown
            bias[tokens : 2 * tokens, side * own_keys : (side + 1) * own_keys] = shown

    def part_copy(tick, j):
        return pltpu.make_async_remote_copy(
            src_ref=sent.at[tick, j],
            dst_ref=arrived.at[tick, chip],
            send_sem=part_send_sem.at[tick, j],
            recv_sem=part_recv_sem.at[tick, chip],
            device_id=in_section(j),
            device_id_type=MESH,
        )

    def stat_copy(tick, j):
        return pltpu.make_async_remote_copy(
            src_ref=sent_stats.at[tick, j],
            dst_ref=arrived_stats.at[tick, chip],
            send_sem=stat_send_sem.at[tick, j],
            recv_sem=stat_recv_sem.at[tick, chip],
            device_id=in_section(j),
            device_id_type=MESH,
        )

    def part_arrival(tick, j):
        return pltpu.make_async_remote_copy(
            src_ref=sent.at[tick, j],
            dst_ref=arrived.at[tick, j],
            send_sem=part_send_sem.at[tick, j],
            recv_sem=part_recv_sem.at[tick, j],
            device_id=in_section(j),
            device_id_type=MESH,
        )

    def stat_arrival(tick, j):
        return pltpu.make_async_remote_copy(
            src_ref=sent_stats.at[tick, j],
            dst_ref=arrived_stats.at[tick, j],
            send_sem=stat_send_sem.at[tick, j],
            recv_sem=stat_recv_sem.at[tick, j],
            device_id=in_section(j),
            device_id_type=MESH,
        )

    def attend(tick, h, hidden):
        head_gain = gain[:, columns(h, GROUP * HD)]
        rows = []
        for g in range(GROUP):
            x = hidden[:, g * HD : (g + 1) * HD]
            mean = jnp.mean(x * x, axis=1, keepdims=True)
            rows.append(x * lax.rsqrt(mean + EPSILON) * head_gain[:, g * HD : (g + 1) * HD])
        queries = jnp.concatenate(rows, axis=0).astype(jnp.bfloat16)
        scores[...] = lax.dot_general(
            queries, keys[h], (((1,), (1,)), ((), ())), preferred_element_type=jnp.float32
        )
        block = 2 * tokens
        maxima = []
        for g in range(GROUP * tokens // block):
            part = scores[g * block : (g + 1) * block, :] + bias[...]
            top = jnp.max(part, axis=1, keepdims=True)
            maxima.append(top)
            probs[g * block : (g + 1) * block, :] = jnp.exp2(
                (part - top) * EXPONENT_SCALE
            ).astype(jnp.bfloat16)
        top = jnp.concatenate(maxima, axis=0)
        product = lax.dot_general(
            probs[...], values[h], (((1,), (0,)), ((), ())), preferred_element_type=jnp.float32
        )
        lanes = lax.broadcasted_iota(jnp.int32, (chunk_rows, HD), 1)
        for q in range(chunks_per_head):
            j = h * chunks_per_head + q
            span = slice(q * chunk_rows, (q + 1) * chunk_rows)
            weighted = product[span, :HD].astype(jnp.bfloat16)
            stats = jnp.where(lanes == 0, top[span], product[span, HD:])
            stats = jnp.concatenate(
                [stats, jnp.ones((HD - chunk_rows, HD), jnp.float32)], axis=0
            )
            stats = stats.T[0:8]

            @pl.when(j == chip)
            def _(weighted=weighted, stats=stats):
                arrived[tick, chip] = weighted
                arrived_stats[tick, chip] = stats

            @pl.when(j != chip)
            def _(j=j, weighted=weighted, stats=stats):
                sent[tick, j] = weighted
                sent_stats[tick, j] = stats
                part_copy(tick, j).start()
                stat_copy(tick, j).start()

    def combine(tick, residual):
        @pl.loop(0, n_chips)
        def _(j):
            @pl.when(j != chip)
            def _():
                part_arrival(tick, j).wait()
                stat_arrival(tick, j).wait()

        tops = arrived_stats[tick, :, 0, :]
        totals = arrived_stats[tick, :, 1, :]
        overall = jnp.max(tops, axis=0, keepdims=True)
        factors = jnp.exp2((tops - overall) * EXPONENT_SCALE)
        factors = factors / jnp.sum(factors * totals, axis=0, keepdims=True)
        factors = jnp.concatenate(
            [factors, jnp.zeros((HD - n_chips, HD), jnp.float32)], axis=0
        ).T
        attended = jnp.zeros((chunk_rows, HD), jnp.float32)
        for j in range(n_chips):
            attended += factors[:chunk_rows, j : j + 1] * arrived[tick, j].astype(jnp.float32)
        for g in range(heads_in_chunk):
            lanes = slice(g * HD, (g + 1) * HD)
            combined[tick, :, lanes] = (
                residual[:, lanes] + attended[g * tokens : (g + 1) * tokens]
            ).astype(jnp.bfloat16)

    set_bias(act_frames[pl.ds(section, 1), :])

    @pl.loop(0, kv_heads)
    def _(i):
        h = visit(i)
        for copy in own_copies(h):
            copy.wait()
        for copy in pair_arrivals(h):
            copy.wait_recv()
        for copy in pair_copies(h):
            copy.wait_send()
        attend(0, h, act[:, columns(h, GROUP * HD)].astype(jnp.float32))

    combine(0, act[:, columns(chip, chunk_columns)].astype(jnp.float32))

    def hand_copy(j):
        return pltpu.make_async_remote_copy(
            src_ref=combined.at[0],
            dst_ref=handed.at[:, columns(chip, chunk_columns)],
            send_sem=hand_send_sem.at[j],
            recv_sem=hand_recv_sem.at[chip],
            device_id=(following, j * 2 + core),
            device_id_type=MESH,
        )

    def hand_arrival(j):
        return pltpu.make_async_remote_copy(
            src_ref=combined.at[0],
            dst_ref=handed.at[:, columns(j, chunk_columns)],
            send_sem=hand_send_sem.at[j],
            recv_sem=hand_recv_sem.at[j],
            device_id=(previous, j * 2 + core),
            device_id_type=MESH,
        )

    @pl.loop(0, n_chips)
    def _(k):
        hand_copy((chip + n_chips // 2 + k) % n_chips).start()

    first = section == 0
    set_bias(jnp.where(first, fresh_frames[...], act_frames[pl.ds(previous, 1), :]))

    def incoming(span):
        return jnp.where(
            first, fresh[:, span].astype(jnp.float32), handed[:, span].astype(jnp.float32)
        )

    @pl.loop(0, kv_heads)
    def _(i):
        h = visit(i)
        for q in range(chunks_per_head):
            hand_arrival(h * chunks_per_head + q).wait_recv()
        attend(1, h, incoming(columns(h, GROUP * HD)))

    combine(1, incoming(columns(chip, chunk_columns)))

    def result_columns(half, j):
        return pl.ds(pl.multiple_of(half * plane + j * chunk_columns, chunk_columns), chunk_columns)

    def out_copy(j):
        return pltpu.make_async_remote_copy(
            src_ref=combined.at[1],
            dst_ref=out_ref.at[:, result_columns(core, chip)],
            send_sem=out_send_sem.at[j],
            recv_sem=out_recv_sem.at[chip],
            device_id=in_section(j),
            device_id_type=MESH,
        )

    def out_arrival(j):
        return pltpu.make_async_remote_copy(
            src_ref=combined.at[1],
            dst_ref=out_ref.at[:, result_columns(core, j)],
            send_sem=out_send_sem.at[j],
            recv_sem=out_recv_sem.at[j],
            device_id=in_section(j),
            device_id_type=MESH,
        )

    def cross_copy(j, half):
        return pltpu.make_async_remote_copy(
            src_ref=out_ref.at[:, result_columns(half, j)],
            dst_ref=out_ref.at[:, result_columns(half, j)],
            send_sem=cross_send_sem.at[j],
            recv_sem=cross_recv_sem.at[j],
            device_id=sibling,
            device_id_type=MESH,
        )

    @pl.loop(0, n_chips)
    def _(k):
        j = (chip + n_chips // 2 + k) % n_chips

        @pl.when(j != chip)
        def _():
            out_copy(j).start()

    out_ref[:, result_columns(core, chip)] = combined[1]
    cross_copy(chip, core).start()

    @pl.loop(1, n_chips)
    def _(k):
        away = (k + 1) // 2
        j = (chip + jnp.where(k % 2 == 1, away, n_chips - away)) % n_chips
        out_arrival(j).wait_recv()
        cross_copy(j, core).start()

    @pl.loop(0, n_chips)
    def _(j):
        cross_copy(j, other).wait_recv()
        cross_copy(j, core).wait_send()
        hand_copy(j).wait_send()

        @pl.when(j != chip)
        def _():
            out_copy(j).wait_send()


def attention(n_sections, n_chips, act, act_frames, fresh, fresh_frames, gain, keys, values, key_frames):
    tokens, width = act.shape
    own_keys = keys.shape[0]
    plane = width // 2
    kv_heads = plane // (GROUP * HD)
    chunk_columns = plane // n_chips
    chunk_rows = chunk_columns // HD * tokens
    dma = pltpu.SemaphoreType.DMA
    anywhere = pl.BlockSpec(memory_space=pl.ANY)
    return pl.pallas_call(
        functools.partial(kernel, n_sections, n_chips),
        out_shape=jax.ShapeDtypeStruct((tokens, width), jnp.bfloat16),
        in_specs=[anywhere] * 8,
        out_specs=pl.BlockSpec(memory_space=pltpu.VMEM),
        scratch_shapes=[
            pltpu.VMEM((tokens, plane), jnp.bfloat16),
            pltpu.VMEM((tokens, plane), jnp.bfloat16),
            pltpu.VMEM(act_frames.shape, jnp.int32),
            pltpu.VMEM(fresh_frames.shape, jnp.int32),
            pltpu.VMEM((1, plane), jnp.float32),
            pltpu.VMEM((2, 1, own_keys), jnp.int32),
            pltpu.VMEM((kv_heads, 2 * own_keys, HD), jnp.bfloat16),
            pltpu.VMEM((kv_heads, 2 * own_keys, 2 * HD), jnp.bfloat16),
            pltpu.VMEM((2 * tokens, 2 * own_keys), jnp.float32),
            pltpu.VMEM((GROUP * tokens, 2 * own_keys), jnp.float32),
            pltpu.VMEM((GROUP * tokens, 2 * own_keys), jnp.bfloat16),
            pltpu.VMEM((2, n_chips, chunk_rows, HD), jnp.bfloat16),
            pltpu.VMEM((2, n_chips, 8, HD), jnp.float32),
            pltpu.VMEM((2, n_chips, chunk_rows, HD), jnp.bfloat16),
            pltpu.VMEM((2, n_chips, 8, HD), jnp.float32),
            pltpu.VMEM((2, tokens, chunk_columns), jnp.bfloat16),
            pltpu.VMEM((tokens, plane), jnp.bfloat16),
            dma((6,)),
            dma((kv_heads,)),
            dma((kv_heads,)),
            dma((kv_heads, 2)),
            dma((kv_heads, 2)),
            dma,
            dma,
            dma((2, n_chips)),
            dma((2, n_chips)),
            dma((2, n_chips)),
            dma((2, n_chips)),
            dma((n_chips,)),
            dma((n_chips,)),
            dma((n_chips,)),
            dma((n_chips,)),
            dma((n_chips,)),
            dma((n_chips,)),
        ],
        compiler_params=pltpu.CompilerParams(
            collective_id=0, has_side_effects=True, vmem_limit_bytes=40 * 2**20
        ),
        name="two_ticks",
    )(act, act_frames, fresh, fresh_frames, gain, keys, values, key_frames)


def solution(mesh):
    n_sections, n_chips = mesh.shape["section"], mesh.shape["ctx"] // 2

    def body(act, act_frames, fresh, fresh_frames, gain, keys, values, key_frames):
        result = attention(
            n_sections,
            n_chips,
            act[0],
            act_frames,
            fresh,
            fresh_frames[None],
            gain,
            keys[0],
            values[0],
            key_frames[None],
        )
        return result[None]

    placed = (
        P("section", None, None),
        P(),
        P(),
        P(),
        P("section", None),
        P("section", "ctx", None),
        P("section", "ctx", None),
        P("ctx"),
    )
    return jax.shard_map(
        body, mesh=mesh, in_specs=placed, out_specs=P("section", None, None), check_vma=False
    )
```

time: 416 us -> 71 us (0.17)
  blocking collectives: 193 us -> 0 us
  waiting for transfers between devices: 174 us -> 0 us
  Pallas kernels: 0 us -> 62.1 us
  other arithmetic: 15.8 us -> 0 us
  between operations: 13.7 us -> 0.02 us
  matrix products: 9.26 us -> 0 us
    psum x2 -> x0, waiting for transfers between devices: 166 us -> none  [layer(): lax.psum((factors * partials[1], factors[..., None] * partials[2]), 'ctx')]
    pmax x2 -> x0, blocking collectives: 101 us -> none  [layer(): overall = lax.pmax(partials[0], 'ctx')]
    psum x2 -> x0, blocking collectives: 91.5 us -> none  [layer(): lax.psum((factors * partials[1], factors[..., None] * partials[2]), 'ctx')]
    pallas_call x0 -> x1, Pallas kernels: none -> 62.1 us  [attention(): pl.pallas_call(functools.partial(kernel, n_sections, n_chips), out_shape=...]
    dot_general x4 -> x0, matrix products: 9.26 us -> none  [the longest x2 4.74 us: partial_terms(): jnp.einsum('tkgd,jkd->tkgj', grouped, key_rows, preferred_element_type=jn...]
    ppermute x1 -> x0, waiting for transfers between devices: 7.44 us -> none  [passed_along(): return lax.ppermute(block, axis, route)]
    reduce_sum x4 -> x0, other arithmetic: 6.56 us -> none  [the longest x2 6.01 us: partial_terms(): totals = jnp.sum(probabilities.astype(jnp.float32), axis=-1)]
  transfers between devices with their start and end apart: 3 -> 0, of which waited for: 3 -> 0; matrix products, arithmetic and copies ran while one was open for 0% -> 0% of each run, Pallas kernels for 0% -> 0%
where the time goes in v1:
time: 71 us; the launch traced here: 70.6 us
  Pallas kernels  62.1 us (87%)
  local copies, waits for them, and re-layouts  8.44 us (12%)
    pallas_call x1, Pallas kernels, attention(): pl.pallas_call(functools.partial(kernel, n_sections, n_chips), out_shape=...  62.1 us
    unnamed x14, local copies, waits for them, and re-layouts  7.75 us

profile of v1, /device:TPU:1, one launch (start us, length us, event | category | flops | bytes accessed | tf_op | source)
XLA Modules:
  0.0 70.6 jit_solution(3057502263780022803)
XLA Ops:
  0.0 0.7 broadcast_in_dim.10.key_frames_hbm
  0.7 0.8 %copy.9.act_frames_hbm = s32[64,24]{1,0:T(8,128)S(1)} copy(s32[64,24]{0,1:T(8,128)} %param.9) | data formatting | bytes 12288 | tf_op args[1]
  1.5 0.0 copy-start
  1.5 1.4 %copy-done = bf16[1,768,1024]{2,1,0:T(8,128)(2,1)S(1)} copy-done((bf16[1,768,1024]{2,1,0:T(8,128)(2,1)S(1)}, bf16[1,768,1024]{2,1,0:T(8,128)(2,1)}, u32[]{:S(2)}) %copy-start) | copy-done | bytes 1572888
  2.9 0.0 copy-start.1
  2.9 1.4 %copy-done.1 = bf16[1,768,1024]{2,1,0:T(8,128)(2,1)S(1)} copy-done((bf16[1,768,1024]{2,1,0:T(8,128)(2,1)S(1)}, bf16[1,768,1024]{2,1,0:T(8,128)(2,1)}, u32[]{:S(2)}) %copy-start.1) | copy-done | bytes 1572888
  4.3 0.0 copy-start.2
  4.3 1.0 %copy-done.2 = bf16[1,24,8192]{2,1,0:T(8,128)(2,1)S(1)} copy-done((bf16[1,24,8192]{2,1,0:T(8,128)(2,1)S(1)}, bf16[1,24,8192]{2,1,0:T(8,128)(2,1)}, u32[]{:S(2)}) %copy-start.2) | copy-done | bytes 393240
  5.3 0.0 copy-start.3
  5.3 1.0 %copy-done.3 = bf16[24,8192]{1,0:T(8,128)(2,1)S(1)} copy-done((bf16[24,8192]{1,0:T(8,128)(2,1)S(1)}, bf16[24,8192]{1,0:T(8,128)(2,1)}, u32[]{:S(2)}) %copy-start.3) | copy-done | bytes 393240
  6.3 0.0 copy-start.4
  6.3 0.8 %copy-done.4 = f32[1,8192]{1,0:T(1,128)S(1)} copy-done((f32[1,8192]{1,0:T(1,128)S(1)}, f32[1,8192]{1,0:T(1,128)}, u32[]{:S(2)}) %copy-start.4) | copy-done | bytes 32792
  7.0 0.0 copy-start.5
  7.0 0.7 copy-done.5
  7.7 62.1 %two_ticks.1 = bf16[24,8192]{1,0:T(8,128)(2,1)S(1)} custom-call(bf16[24,8192]{1,0:T(8,128)(2,1)S(1)} %bitcast.8, s32[64,24]{1,0:T(8,128)S(1)} %copy.9.act_frames_hbm, bf16[24,8192]{1,0:T(8,128)(2,1)S(1)} %copy-done.3, s32[1,24]{1,0:T(1,128)S(1)} %bitcast.9, f32[1,8192]{1,0:T(1,128)S(1)} %copy-done.4, bf16[768,1024]{1,0:T(8,128)(2,1)S(1)} %bitcast.5, ...), custom_call_target="tpu_custom_call" | custom-call | tf_op jit(solution)/shard_map/two_ticks/pallas_call | solution.py:450
  69.8 0.7 %copy.11 = bf16[1,24,8192]{2,1,0:T(8,128)(2,1)} copy(bf16[1,24,8192]{2,1,0:T(8,128)(2,1)S(1)} %bitcast.7) | data formatting | bytes 786432
Async XLA Ops:
  1.5 1.4 %copy-start = (bf16[1,768,1024]{2,1,0:T(8,128)(2,1)S(1)}, bf16[1,768,1024]{2,1,0:T(8,128)(2,1)}, u32[]{:S(2)}) copy-start(bf16[1,768,1024]{2,1,0:T(8,128)(2,1)} %param.13) | copy-start | bytes 4718596
  2.9 1.4 %copy-start.1 = (bf16[1,768,1024]{2,1,0:T(8,128)(2,1)S(1)}, bf16[1,768,1024]{2,1,0:T(8,128)(2,1)}, u32[]{:S(2)}) copy-start(bf16[1,768,1024]{2,1,0:T(8,128)(2,1)} %param.14) | copy-start | bytes 4718596
  4.3 1.0 %copy-start.2 = (bf16[1,24,8192]{2,1,0:T(8,128)(2,1)S(1)}, bf16[1,24,8192]{2,1,0:T(8,128)(2,1)}, u32[]{:S(2)}) copy-start(bf16[1,24,8192]{2,1,0:T(8,128)(2,1)} %param.8) | copy-start | bytes 1179652
  5.3 1.0 %copy-start.3 = (bf16[24,8192]{1,0:T(8,128)(2,1)S(1)}, bf16[24,8192]{1,0:T(8,128)(2,1)}, u32[]{:S(2)}) copy-start(bf16[24,8192]{1,0:T(8,128)(2,1)} %fresh_hbm.1) | copy-start | bytes 1179652
  6.3 0.8 %copy-start.4 = (f32[1,8192]{1,0:T(1,128)S(1)}, f32[1,8192]{1,0:T(1,128)}, u32[]{:S(2)}) copy-start(f32[1,8192]{1,0:T(1,128)} %gain_hbm.1) | copy-start | bytes 98308
  7.0 0.7 copy-start.5

commit v2 on v0

v2 whole, which is shorter than its diff:
```python
import functools
import math

import jax
import jax.numpy as jnp
from jax import lax
from jax.experimental import pallas as pl
from jax.experimental.pallas import tpu as pltpu
from jax.sharding import PartitionSpec as P

HD = 128
GROUP = 8
EPSILON = 1e-05
MASKED = -1e30
MESH = pl.DeviceIdType.MESH
EXPONENT_SCALE = HD**-0.5 * math.log2(math.e)
STAT_ROWS = 16


def frames_stride(count):
    return -(-count // 1024) * 1024


def remote(src, dst, send_sem, recv_sem, device):
    return pltpu.make_async_remote_copy(
        src_ref=src,
        dst_ref=dst,
        send_sem=send_sem,
        recv_sem=recv_sem,
        device_id=device,
        device_id_type=MESH,
    )


def kernel(
    n_sections,
    n_chips,
    act_hbm,
    act_frames_hbm,
    fresh_hbm,
    fresh_frames_hbm,
    gain_hbm,
    keys_hbm,
    values_hbm,
    key_frames_hbm,
    out_ref,
    act,
    fresh,
    act_frames,
    fresh_frames,
    gain,
    key_frames,
    keys,
    values,
    bias,
    parts,
    pair_arrived,
    sent,
    arrived,
    combined,
    handed,
    local_sem,
    keys_sem,
    values_sem,
    pair_send_sem,
    pair_recv_sem,
    cache_send_sem,
    cache_recv_sem,
    frames_send_sem,
    frames_recv_sem,
    part_send_sem,
    part_recv_sem,
    hand_send_sem,
    hand_recv_sem,
    out_send_sem,
    out_recv_sem,
    cross_send_sem,
    cross_recv_sem,
    line_sem,
):
    tokens = act.shape[0]
    own_keys = keys_hbm.shape[0]
    plane = fresh.shape[1]
    kv_heads = plane // (GROUP * HD)
    head_rows = GROUP * tokens
    chunk_columns = plane // n_chips
    heads_in_chunk = chunk_columns // HD
    chunk_rows = heads_in_chunk * tokens
    chunks_per_head = head_rows // chunk_rows

    section = lax.axis_index("section")
    ctx = lax.axis_index("ctx")
    chip, core = ctx // 2, ctx % 2
    other = 1 - core
    sibling = (section, chip * 2 + other)
    not_first = section != 0
    not_last = section != n_sections - 1

    def in_line(j):
        return (section, j * 2 + core)

    def columns(j, width):
        return pl.ds(pl.multiple_of(j * width, width), width)

    def far_first(k):
        half = n_chips // 2
        step = jnp.where(k % 2 == 1, half - (k + 1) // 2, half + k // 2)
        return (chip + step) % n_chips

    def slot_of(i, h):
        return jnp.where(i < kv_heads, 2 * kv_heads + h, 2 * h + core)

    def visit(i):
        i = i % kv_heads
        step = jnp.where(i == 0, 2, jnp.where(i == 1, 1, jnp.where(i == 2, 3, 0)))
        return (chip // chunks_per_head + step) % kv_heads

    def loads(i):
        h = visit(i)
        half = jnp.where(i < kv_heads, other, core)
        span = columns(half * kv_heads + h, HD)
        slot = slot_of(i, h)
        return (
            pltpu.make_async_copy(keys_hbm.at[:, span], keys.at[slot], keys_sem.at[i]),
            pltpu.make_async_copy(
                values_hbm.at[:, span], values.at[slot, :, pl.ds(0, HD)], values_sem.at[i]
            ),
        )

    stride = frames_stride(own_keys)
    own_frames = pl.ds(pl.multiple_of(core * stride, stride), own_keys)
    small = [
        pltpu.make_async_copy(act_hbm, act, local_sem.at[0]),
        pltpu.make_async_copy(act_frames_hbm, act_frames, local_sem.at[1]),
        pltpu.make_async_copy(gain_hbm, gain, local_sem.at[2]),
        pltpu.make_async_copy(key_frames_hbm, key_frames.at[own_frames], local_sem.at[3]),
    ]
    late = [
        pltpu.make_async_copy(fresh_hbm.at[:, columns(core, plane)], fresh, local_sem.at[4]),
        pltpu.make_async_copy(fresh_frames_hbm, fresh_frames, local_sem.at[5]),
    ]
    for copy in small:
        copy.start()

    barrier = pltpu.get_barrier_semaphore()
    pl.semaphore_signal(barrier, inc=1, device_id=sibling, device_id_type=MESH)

    @pl.loop(0, n_chips - 1)
    def _(k):
        pl.semaphore_signal(barrier, inc=1, device_id=in_line(far_first(k)), device_id_type=MESH)

    @pl.when(not_first)
    def _():
        pl.semaphore_signal(barrier, inc=1, device_id=(section - 1, ctx), device_id_type=MESH)

    @pl.when(not_last)
    def _():
        pl.semaphore_signal(barrier, inc=1, device_id=(section + 1, ctx), device_id_type=MESH)

    for i in range(2 * kv_heads):
        for copy in loads(i):
            copy.start()
    for copy in late:
        copy.start()
    for slot in range(values.shape[0]):
        values[slot, :, HD:] = jnp.ones((own_keys, HD), values.dtype)
    for copy in small:
        copy.wait()

    def held_frames(s):
        lanes = lax.broadcasted_iota(jnp.int32, act_frames.shape, 1)
        spread = act_frames[...].astype(jnp.float32)
        return jnp.sum(jnp.where(lanes == s, spread, 0.0), axis=1, keepdims=True)

    def entering_frames():
        rows = lax.broadcasted_iota(jnp.int32, (tokens, tokens), 0)
        lanes = lax.broadcasted_iota(jnp.int32, (tokens, tokens), 1)
        spread = jnp.broadcast_to(fresh_frames[...], (tokens, tokens)).astype(jnp.float32)
        return jnp.sum(jnp.where(rows == lanes, spread, 0.0), axis=1, keepdims=True)

    def shown(frames, column):
        row = key_frames[frames].astype(jnp.float32)[None]
        return jnp.where(row <= column, 0.0, MASKED)

    def queries_of(hidden, head_gain):
        rows = []
        for g in range(GROUP):
            span = slice(g * HD, (g + 1) * HD)
            x = hidden[:, span]
            mean = jnp.mean(x * x, axis=1, keepdims=True)
            rows.append(x * lax.rsqrt(mean + EPSILON) * head_gain[:, span])
        return jnp.concatenate(rows, axis=0).astype(jnp.bfloat16)

    def attend(queries, head_keys, head_values, mask):
        scores = lax.dot_general(
            queries, head_keys, (((1,), (1,)), ((), ())), preferred_element_type=jnp.float32
        )
        block = 2 * tokens
        maxima, probs = [], []
        for g in range(head_rows // block):
            part = scores[g * block : (g + 1) * block] + mask
            top = jnp.max(part, axis=1, keepdims=True)
            maxima.append(top)
            probs.append(jnp.exp2((part - top) * EXPONENT_SCALE).astype(jnp.bfloat16))
        product = lax.dot_general(
            jnp.concatenate(probs, axis=0),
            head_values,
            (((1,), (0,)), ((), ())),
            preferred_element_type=jnp.float32,
        )
        return jnp.concatenate(maxima, axis=0), product

    def part_copy(tick, j):
        return remote(
            sent.at[tick, j],
            arrived.at[tick, chip],
            part_send_sem.at[tick, j],
            part_recv_sem.at[tick, chip],
            in_line(j),
        )

    def part_arrival(tick, j):
        return remote(
            sent.at[tick, j],
            arrived.at[tick, j],
            part_send_sem.at[tick, j],
            part_recv_sem.at[tick, j],
            in_line(j),
        )

    def ship(tick, h, top, totals, weighted):
        lanes = lax.broadcasted_iota(jnp.int32, (chunk_rows, HD), 1)
        for q in range(chunks_per_head):
            j = h * chunks_per_head + q
            span = slice(q * chunk_rows, (q + 1) * chunk_rows)
            stats = jnp.where(lanes % 2 == 0, top[span], totals[span])
            high = stats.astype(jnp.bfloat16).astype(jnp.float32)
            middle = (stats - high).astype(jnp.bfloat16).astype(jnp.float32)
            low = stats - high - middle
            terms = jnp.where(lanes < 2, high, jnp.where(lanes < 4, middle, low))
            terms = jnp.concatenate(
                [terms, jnp.ones((HD - chunk_rows, HD), jnp.float32)], axis=0
            ).T[:STAT_ROWS]
            packet = jnp.concatenate([weighted[span], terms], axis=0).astype(jnp.bfloat16)

            @pl.when(j == chip)
            def _(packet=packet):
                arrived[tick, chip] = packet

            @pl.when(j != chip)
            def _(j=j, packet=packet):
                sent[tick, j] = packet
                part_copy(tick, j).start()

    def combine(tick, residual):
        @pl.loop(0, n_chips)
        def _(j):
            @pl.when(j != chip)
            def _():
                part_arrival(tick, j).wait()

        stats = arrived[tick, :, chunk_rows:, :].astype(jnp.float32)
        tops = stats[:, 0] + stats[:, 2] + stats[:, 4]
        totals = stats[:, 1] + stats[:, 3] + stats[:, 5]
        overall = jnp.max(tops, axis=0, keepdims=True)
        factors = jnp.exp2((tops - overall) * EXPONENT_SCALE)
        factors = factors / jnp.sum(factors * totals, axis=0, keepdims=True)
        factors = jnp.concatenate(
            [factors, jnp.zeros((HD - n_chips, HD), jnp.float32)], axis=0
        ).T
        attended = jnp.zeros((chunk_rows, HD), jnp.float32)
        for j in range(n_chips):
            weighted = arrived[tick, j, :chunk_rows].astype(jnp.float32)
            attended += factors[:chunk_rows, j : j + 1] * weighted
        for g in range(heads_in_chunk):
            lanes = slice(g * HD, (g + 1) * HD)
            combined[tick, :, lanes] = (
                residual[:, lanes] + attended[g * tokens : (g + 1) * tokens]
            ).astype(jnp.bfloat16)

    mask = shown(own_frames, held_frames(section))
    bias[0:tokens, 0:own_keys] = mask
    bias[tokens : 2 * tokens, 0:own_keys] = mask
    pair_lanes = lax.broadcasted_iota(jnp.int32, (head_rows, HD), 1)

    def first_tick(i):
        h = visit(i)
        half = jnp.where(i < kv_heads, other, core)
        span = columns(half * kv_heads + h, GROUP * HD)
        for copy in loads(i):
            copy.wait()
        slot = slot_of(i, h)
        queries = queries_of(act[:, span].astype(jnp.float32), gain[:, span])
        top, product = attend(queries, keys[slot], values[slot], bias[:, 0:own_keys])
        place = jnp.where(i < kv_heads, h, kv_heads + h)
        parts[place, :, :HD] = product[:, :HD]
        parts[place, :, HD:] = jnp.where(pair_lanes < HD // 2, top, product[:, HD:])

    @pl.loop(0, 2 * kv_heads - 2)
    def _(i):
        first_tick(i)

    pl.semaphore_wait(barrier, n_chips + not_first.astype(jnp.int32) + not_last.astype(jnp.int32))

    def pair_copy(h):
        return remote(
            parts.at[h], pair_arrived.at[h], pair_send_sem.at[h], pair_recv_sem.at[h], sibling
        )

    @pl.loop(0, kv_heads)
    def _(i):
        pair_copy(visit(i)).start()

    frames_copy = remote(
        key_frames_hbm, key_frames.at[own_frames], frames_send_sem, frames_recv_sem, sibling
    )
    frames_copy.start()

    @pl.when(not_first)
    def _():
        pl.semaphore_signal(line_sem, inc=1, device_id=(section - 1, ctx), device_id_type=MESH)

    @pl.loop(2 * kv_heads - 2, 2 * kv_heads)
    def _(i):
        first_tick(i)

    @pl.loop(0, kv_heads)
    def _(i):
        h = visit(i)
        pair_copy(h).wait()
        own_top = parts[kv_heads + h, :, HD : HD + 1]
        own_totals = parts[kv_heads + h, :, 2 * HD - 1 :]
        pair_top = pair_arrived[h, :, HD : HD + 1]
        pair_totals = pair_arrived[h, :, 2 * HD - 1 :]
        top = jnp.maximum(own_top, pair_top)
        own_factor = jnp.exp2((own_top - top) * EXPONENT_SCALE)
        pair_factor = jnp.exp2((pair_top - top) * EXPONENT_SCALE)
        totals = own_factor * own_totals + pair_factor * pair_totals
        weighted = (
            own_factor * parts[kv_heads + h, :, :HD] + pair_factor * pair_arrived[h, :, :HD]
        )
        ship(0, h, top, totals, weighted)

    def cache_copies(h):
        from_slot, to_slot = 2 * kv_heads + h, 2 * h + core
        return (
            remote(
                keys.at[from_slot],
                keys.at[to_slot],
                cache_send_sem.at[h, 0],
                cache_recv_sem.at[h, 0],
                sibling,
            ),
            remote(
                values.at[from_slot, :, pl.ds(0, HD)],
                values.at[to_slot, :, pl.ds(0, HD)],
                cache_send_sem.at[h, 1],
                cache_recv_sem.at[h, 1],
                sibling,
            ),
        )

    def cache_arrivals(h):
        from_slot, to_slot = 2 * kv_heads + h, 2 * h + other
        return (
            remote(
                keys.at[from_slot],
                keys.at[to_slot],
                cache_send_sem.at[h, 0],
                cache_recv_sem.at[h, 0],
                sibling,
            ),
            remote(
                values.at[from_slot, :, pl.ds(0, HD)],
                values.at[to_slot, :, pl.ds(0, HD)],
                cache_send_sem.at[h, 1],
                cache_recv_sem.at[h, 1],
                sibling,
            ),
        )

    for h in range(kv_heads):
        for copy in cache_copies(h):
            copy.start()

    for copy in late:
        copy.wait()
    frames_copy.wait()
    column = jnp.where(not_first, held_frames(section - 1), entering_frames())
    for side in range(2):
        mask = shown(pl.ds(side * stride, own_keys), column)
        span = slice(side * own_keys, (side + 1) * own_keys)
        bias[0:tokens, span] = mask
        bias[tokens : 2 * tokens, span] = mask

    combine(0, act[:, columns(core * n_chips + chip, chunk_columns)].astype(jnp.float32))

    def hand_copy(j):
        return remote(
            combined.at[0],
            handed.at[:, columns(chip, chunk_columns)],
            hand_send_sem.at[j],
            hand_recv_sem.at[chip],
            (section + 1, j * 2 + core),
        )

    def hand_arrival(j):
        return remote(
            combined.at[0],
            handed.at[:, columns(j, chunk_columns)],
            hand_send_sem.at[j],
            hand_recv_sem.at[j],
            (section - 1, j * 2 + core),
        )

    @pl.when(not_last)
    def _():
        pl.semaphore_wait(line_sem, 1)

        @pl.loop(0, n_chips)
        def _(k):
            hand_copy(far_first(k)).start()

    def incoming(span):
        return jnp.where(
            not_first, handed[:, span].astype(jnp.float32), fresh[:, span].astype(jnp.float32)
        )

    for h in range(kv_heads):
        for copy in cache_arrivals(h):
            copy.wait()

    @pl.loop(0, kv_heads)
    def _(i):
        h = (chip // chunks_per_head + i) % kv_heads

        @pl.when(not_first)
        def _():
            for q in range(chunks_per_head):
                hand_arrival(h * chunks_per_head + q).wait_recv()

        span = columns(h, GROUP * HD)
        head_gain = gain[:, columns(core * kv_heads + h, GROUP * HD)]
        both = pl.ds(2 * h, 2)
        top, product = attend(
            queries_of(incoming(span), head_gain),
            keys[both].reshape(2 * own_keys, HD),
            values[both].reshape(2 * own_keys, 2 * HD),
            bias[...],
        )
        ship(1, h, top, product[:, HD:], product[:, :HD])

    combine(1, incoming(columns(chip, chunk_columns)))

    def result_columns(half, j):
        return columns(half * n_chips + j, chunk_columns)

    def out_copy(j):
        return remote(
            combined.at[1],
            out_ref.at[:, result_columns(core, chip)],
            out_send_sem.at[j],
            out_recv_sem.at[chip],
            in_line(j),
        )

    def out_arrival(j):
        return remote(
            combined.at[1],
            out_ref.at[:, result_columns(core, j)],
            out_send_sem.at[j],
            out_recv_sem.at[j],
            in_line(j),
        )

    def cross_copy(j, half):
        return remote(
            out_ref.at[:, result_columns(half, j)],
            out_ref.at[:, result_columns(half, j)],
            cross_send_sem.at[j],
            cross_recv_sem.at[j],
            sibling,
        )

    @pl.loop(0, n_chips - 1)
    def _(k):
        out_copy(far_first(k)).start()

    out_ref[:, result_columns(core, chip)] = combined[1]
    cross_copy(chip, core).start()

    @pl.loop(0, n_chips - 1)
    def _(k):
        j = far_first(n_chips - 2 - k)
        out_arrival(j).wait_recv()
        cross_copy(j, core).start()

    @pl.loop(0, n_chips)
    def _(j):
        @pl.when(not_last)
        def _():
            hand_copy(j).wait_send()

        @pl.when(j != chip)
        def _():
            out_copy(j).wait_send()

    @pl.loop(0, n_chips)
    def _(j):
        cross_copy(j, other).wait_recv()
        cross_copy(j, core).wait_send()


def attention(n_sections, n_chips, act, act_frames, fresh, fresh_frames, gain, keys, values, key_frames):
    tokens, width = act.shape
    own_keys = keys.shape[0]
    plane = width // 2
    kv_heads = plane // (GROUP * HD)
    chunk_columns = plane // n_chips
    packet_rows = chunk_columns // HD * tokens + STAT_ROWS
    dma = pltpu.SemaphoreType.DMA
    operands = [
        pltpu.with_memory_space_constraint(x, pltpu.HBM)
        for x in (act, act_frames, fresh, fresh_frames, gain, keys, values, key_frames)
    ]
    return pl.pallas_call(
        functools.partial(kernel, n_sections, n_chips),
        out_shape=jax.ShapeDtypeStruct((tokens, width), jnp.bfloat16),
        in_specs=[pl.BlockSpec(memory_space=pltpu.HBM)] * 8,
        out_specs=pl.BlockSpec(memory_space=pltpu.VMEM),
        scratch_shapes=[
            pltpu.VMEM((tokens, width), jnp.bfloat16),
            pltpu.VMEM((tokens, plane), jnp.bfloat16),
            pltpu.VMEM(act_frames.shape, jnp.int32),
            pltpu.VMEM(fresh_frames.shape, jnp.int32),
            pltpu.VMEM((1, width), jnp.float32),
            pltpu.VMEM((2 * frames_stride(own_keys),), jnp.int32),
            pltpu.VMEM((3 * kv_heads, own_keys, HD), jnp.bfloat16),
            pltpu.VMEM((3 * kv_heads, own_keys, 2 * HD), jnp.bfloat16),
            pltpu.VMEM((2 * tokens, 2 * own_keys), jnp.float32),
            pltpu.VMEM((2 * kv_heads, GROUP * tokens, 2 * HD), jnp.float32),
            pltpu.VMEM((kv_heads, GROUP * tokens, 2 * HD), jnp.float32),
            pltpu.VMEM((2, n_chips, packet_rows, HD), jnp.bfloat16),
            pltpu.VMEM((2, n_chips, packet_rows, HD), jnp.bfloat16),
            pltpu.VMEM((2, tokens, chunk_columns), jnp.bfloat16),
            pltpu.VMEM((tokens, plane), jnp.bfloat16),
            dma((6,)),
            dma((2 * kv_heads,)),
            dma((2 * kv_heads,)),
            dma((kv_heads,)),
            dma((kv_heads,)),
            dma((kv_heads, 2)),
            dma((kv_heads, 2)),
            dma,
            dma,
            dma((2, n_chips)),
            dma((2, n_chips)),
            dma((n_chips,)),
            dma((n_chips,)),
            dma((n_chips,)),
            dma((n_chips,)),
            dma((n_chips,)),
            dma((n_chips,)),
            pltpu.SemaphoreType.REGULAR,
        ],
        compiler_params=pltpu.CompilerParams(
            collective_id=0, has_side_effects=True, vmem_limit_bytes=48 * 2**20
        ),
        name="two_ticks",
    )(*operands)


def solution(mesh):
    n_sections, n_chips = mesh.shape["section"], mesh.shape["ctx"] // 2

    def body(act, act_frames, fresh, fresh_frames, gain, keys, values, key_frames):
        result = attention(
            n_sections,
            n_chips,
            act[0],
            act_frames.T,
            fresh,
            fresh_frames[None],
            gain,
            keys[0],
            values[0],
            key_frames,
        )
        return result[None]

    placed = (
        P("section", None, None),
        P(),
        P(),
        P(),
        P("section", None),
        P("section", "ctx", None),
        P("section", "ctx", None),
        P("ctx"),
    )
    return jax.shard_map(
        body, mesh=mesh, in_specs=placed, out_specs=P("section", None, None), check_vma=False
    )
```

time: 416 us -> 51.3 us (0.12)
  the two profiles are of different devices: /device:TPU:1 before, /device:TPU:3 now
where the time goes in v2:
time: 51.3 us; the launch traced here: 51.1 us
  Pallas kernels  50.4 us (98%)
  local copies, waits for them, and re-layouts  0.75 us (1%)
    pallas_call x1, Pallas kernels, attention(): pl.pallas_call(functools.partial(kernel, n_sections, n_chips), out_shape=...  50.4 us

profile of v2, /device:TPU:3, one launch (start us, length us, event | category | flops | bytes accessed | tf_op | source)
XLA Modules:
  0.0 51.1 jit_solution(11419887134258214205)
XLA Ops:
  0.0 50.4 %two_ticks.1 = bf16[24,8192]{1,0:T(8,128)(2,1)S(1)} custom-call(bf16[24,8192]{1,0:T(8,128)(2,1)} %bitcast.9, s32[24,64]{1,0:T(8,128)} %bitcast.10, bf16[24,8192]{1,0:T(8,128)(2,1)} %fresh_hbm.1, s32[1,24]{1,0:T(1,128)} %bitcast.11, f32[1,8192]{1,0:T(1,128)} %gain_hbm.1, bf16[768,1024]{1,0:T(8,128)(2,1)} %bitcast.7, bf16[768,1024]{1,0:T(8,128)(2,1)} %bitcast.8, ...), custom_call_target="tpu_custom_call" | custom-call | tf_op jit(solution)/shard_map/two_ticks/pallas_call | solution.py:526
  50.4 0.7 %copy.10 = bf16[1,24,8192]{2,1,0:T(8,128)(2,1)} copy(bf16[1,24,8192]{2,1,0:T(8,128)(2,1)S(1)} %bitcast.6) | data formatting | bytes 786432

commit v3 on v2

--- a/solution.py
+++ b/solution.py
@@ -15,6 +15,8 @@
 MESH = pl.DeviceIdType.MESH
 EXPONENT_SCALE = HD**-0.5 * math.log2(math.e)
 STAT_ROWS = 16
+FARTHEST_FIRST = (2, 1, 3, 0)
+NEAREST_FIRST = ((0, 3), (2, 1))
 
 
 def frames_stride(count):
@@ -107,19 +109,16 @@
         step = jnp.where(k % 2 == 1, half - (k + 1) // 2, half + k // 2)
         return (chip + step) % n_chips
 
-    def slot_of(i, h):
-        return jnp.where(i < kv_heads, 2 * kv_heads + h, 2 * h + core)
-
-    def visit(i):
-        i = i % kv_heads
-        step = jnp.where(i == 0, 2, jnp.where(i == 1, 1, jnp.where(i == 2, 3, 0)))
+    def slot_of(own, h):
+        return 2 * h + core if own else 2 * kv_heads + h
+
+    def head_at(step):
         return (chip // chunks_per_head + step) % kv_heads
 
-    def loads(i):
-        h = visit(i)
-        half = jnp.where(i < kv_heads, other, core)
-        span = columns(half * kv_heads + h, HD)
-        slot = slot_of(i, h)
+    def loads(own, step):
+        h = head_at(step)
+        span = columns((core if own else other) * kv_heads + h, HD)
+        slot, i = slot_of(own, h), own * kv_heads + step
         return (
             pltpu.make_async_copy(keys_hbm.at[:, span], keys.at[slot], keys_sem.at[i]),
             pltpu.make_async_copy(
@@ -157,9 +156,10 @@
     def _():
         pl.semaphore_signal(barrier, inc=1, device_id=(section + 1, ctx), device_id_type=MESH)
 
-    for i in range(2 * kv_heads):
-        for copy in loads(i):
-            copy.start()
+    for own in (0, 1):
+        for step in FARTHEST_FIRST:
+            for copy in loads(own, step):
+                copy.start()
     for copy in late:
         copy.start()
     for slot in range(values.shape[0]):
@@ -228,10 +228,11 @@
             in_line(j),
         )
 
-    def ship(tick, h, top, totals, weighted):
+    def ship(tick, step, top, totals, weighted):
+        h = head_at(step)
         lanes = lax.broadcasted_iota(jnp.int32, (chunk_rows, HD), 1)
+        packets = []
         for q in range(chunks_per_head):
-            j = h * chunks_per_head + q
             span = slice(q * chunk_rows, (q + 1) * chunk_rows)
             stats = jnp.where(lanes % 2 == 0, top[span], totals[span])
             high = stats.astype(jnp.bfloat16).astype(jnp.float32)
@@ -241,23 +242,23 @@
             terms = jnp.concatenate(
                 [terms, jnp.ones((HD - chunk_rows, HD), jnp.float32)], axis=0
             ).T[:STAT_ROWS]
-            packet = jnp.concatenate([weighted[span], terms], axis=0).astype(jnp.bfloat16)
-
-            @pl.when(j == chip)
-            def _(packet=packet):
-                arrived[tick, chip] = packet
-
-            @pl.when(j != chip)
-            def _(j=j, packet=packet):
-                sent[tick, j] = packet
+            packets.append(jnp.concatenate([weighted[span], terms], axis=0))
+        if step:
+            for q in range(chunks_per_head):
+                j = h * chunks_per_head + q
+                sent[tick, j] = packets[q].astype(jnp.bfloat16)
                 part_copy(tick, j).start()
+        else:
+            even = chip % 2 == 0
+            arrived[tick, chip] = jnp.where(even, packets[0], packets[1]).astype(jnp.bfloat16)
+            j = chip + jnp.where(even, 1, -1)
+            sent[tick, j] = jnp.where(even, packets[1], packets[0]).astype(jnp.bfloat16)
+            part_copy(tick, j).start()
 
     def combine(tick, residual):
-        @pl.loop(0, n_chips)
-        def _(j):
-            @pl.when(j != chip)
-            def _():
-                part_arrival(tick, j).wait()
+        @pl.loop(0, n_chips - 1)
+        def _(k):
+            part_arrival(tick, far_first(n_chips - 2 - k)).wait()
 
         stats = arrived[tick, :, chunk_rows:, :].astype(jnp.float32)
         tops = stats[:, 0] + stats[:, 2] + stats[:, 4]
@@ -283,23 +284,21 @@
     bias[tokens : 2 * tokens, 0:own_keys] = mask
     pair_lanes = lax.broadcasted_iota(jnp.int32, (head_rows, HD), 1)
 
-    def first_tick(i):
-        h = visit(i)
-        half = jnp.where(i < kv_heads, other, core)
-        span = columns(half * kv_heads + h, GROUP * HD)
-        for copy in loads(i):
-            copy.wait()
-        slot = slot_of(i, h)
-        queries = queries_of(act[:, span].astype(jnp.float32), gain[:, span])
-        top, product = attend(queries, keys[slot], values[slot], bias[:, 0:own_keys])
-        place = jnp.where(i < kv_heads, h, kv_heads + h)
-        parts[place, :, :HD] = product[:, :HD]
-        parts[place, :, HD:] = jnp.where(pair_lanes < HD // 2, top, product[:, HD:])
-
-    @pl.loop(0, 2 * kv_heads - 2)
-    def _(i):
-        first_tick(i)
-
+    def first_tick(own):
+        for step in FARTHEST_FIRST:
+            for copy in loads(own, step):
+                copy.wait()
+        for step in FARTHEST_FIRST:
+            h = head_at(step)
+            span = columns((core if own else other) * kv_heads + h, GROUP * HD)
+            slot = slot_of(own, h)
+            queries = queries_of(act[:, span].astype(jnp.float32), gain[:, span])
+            top, product = attend(queries, keys[slot], values[slot], bias[:, 0:own_keys])
+            place = own * kv_heads + h
+            parts[place, :, :HD] = product[:, :HD]
+            parts[place, :, HD:] = jnp.where(pair_lanes < HD // 2, top, product[:, HD:])
+
+    first_tick(0)
     pl.semaphore_wait(barrier, n_chips + not_first.astype(jnp.int32) + not_last.astype(jnp.int32))
 
     def pair_copy(h):
@@ -307,9 +306,8 @@
             parts.at[h], pair_arrived.at[h], pair_send_sem.at[h], pair_recv_sem.at[h], sibling
         )
 
-    @pl.loop(0, kv_heads)
-    def _(i):
-        pair_copy(visit(i)).start()
+    for step in FARTHEST_FIRST:
+        pair_copy(head_at(step)).start()
 
     frames_copy = remote(
         key_frames_hbm, key_frames.at[own_frames], frames_send_sem, frames_recv_sem, sibling
@@ -320,13 +318,10 @@
     def _():
         pl.semaphore_signal(line_sem, inc=1, device_id=(section - 1, ctx), device_id_type=MESH)
 
-    @pl.loop(2 * kv_heads - 2, 2 * kv_heads)
-    def _(i):
-        first_tick(i)
-
-    @pl.loop(0, kv_heads)
-    def _(i):
-        h = visit(i)
+    first_tick(1)
+
+    for step in FARTHEST_FIRST:
+        h = head_at(step)
         pair_copy(h).wait()
         own_top = parts[kv_heads + h, :, HD : HD + 1]
         own_totals = parts[kv_heads + h, :, 2 * HD - 1 :]
@@ -339,7 +334,7 @@
         weighted = (
             own_factor * parts[kv_heads + h, :, :HD] + pair_factor * pair_arrived[h, :, :HD]
         )
-        ship(0, h, top, totals, weighted)
+        ship(0, step, top, totals, weighted)
 
     def cache_copies(h):
         from_slot, to_slot = 2 * kv_heads + h, 2 * h + core
@@ -430,25 +425,29 @@
         for copy in cache_arrivals(h):
             copy.wait()
 
-    @pl.loop(0, kv_heads)
-    def _(i):
-        h = (chip // chunks_per_head + i) % kv_heads
+    for steps in NEAREST_FIRST:
 
         @pl.when(not_first)
-        def _():
-            for q in range(chunks_per_head):
-                hand_arrival(h * chunks_per_head + q).wait_recv()
-
-        span = columns(h, GROUP * HD)
-        head_gain = gain[:, columns(core * kv_heads + h, GROUP * HD)]
-        both = pl.ds(2 * h, 2)
-        top, product = attend(
-            queries_of(incoming(span), head_gain),
-            keys[both].reshape(2 * own_keys, HD),
-            values[both].reshape(2 * own_keys, 2 * HD),
-            bias[...],
-        )
-        ship(1, h, top, product[:, HD:], product[:, :HD])
+        def _(steps=steps):
+            for step in steps:
+                for q in range(chunks_per_head):
+                    hand_arrival(head_at(step) * chunks_per_head + q).wait_recv()
+
+        results = []
+        for step in steps:
+            h = head_at(step)
+            head_gain = gain[:, columns(core * kv_heads + h, GROUP * HD)]
+            both = pl.ds(2 * h, 2)
+            results.append(
+                attend(
+                    queries_of(incoming(columns(h, GROUP * HD)), head_gain),
+                    keys[both].reshape(2 * own_keys, HD),
+                    values[both].reshape(2 * own_keys, 2 * HD),
+                    bias[...],
+                )
+            )
+        for step, (top, product) in zip(steps, results):
+            ship(1, step, top, product[:, HD:], product[:, :HD])
 
     combine(1, incoming(columns(chip, chunk_columns)))
 

time: 51.3 us -> 51.2 us (level)
  no operation moved by 1% of the time
where the time goes in v3:
time: 51.2 us; the launch traced here: 51 us
  Pallas kernels  50.3 us (98%)
  local copies, waits for them, and re-layouts  0.75 us (1%)
    pallas_call x1, Pallas kernels, attention(): pl.pallas_call(functools.partial(kernel, n_sections, n_chips), out_shape=...  50.3 us

profile of v3, /device:TPU:3, one launch (start us, length us, event | category | flops | bytes accessed | tf_op | source)
XLA Modules:
  0.0 51.0 jit_solution(3666959334914625391)
XLA Ops:
  0.0 50.3 %two_ticks.1 = bf16[24,8192]{1,0:T(8,128)(2,1)S(1)} custom-call(bf16[24,8192]{1,0:T(8,128)(2,1)} %bitcast.9, s32[24,64]{1,0:T(8,128)} %bitcast.10, bf16[24,8192]{1,0:T(8,128)(2,1)} %fresh_hbm.1, s32[1,24]{1,0:T(1,128)} %bitcast.11, f32[1,8192]{1,0:T(1,128)} %gain_hbm.1, bf16[768,1024]{1,0:T(8,128)(2,1)} %bitcast.7, bf16[768,1024]{1,0:T(8,128)(2,1)} %bitcast.8, ...), custom_call_target="tpu_custom_call" | custom-call | tf_op jit(solution)/shard_map/two_ticks/pallas_call | solution.py:525
  50.3 0.7 %copy.10 = bf16[1,24,8192]{2,1,0:T(8,128)(2,1)} copy(bf16[1,24,8192]{2,1,0:T(8,128)(2,1)S(1)} %bitcast.6) | data formatting | bytes 786432

commit v4 on v3

--- a/solution.py
+++ b/solution.py
@@ -16,7 +16,7 @@
 EXPONENT_SCALE = HD**-0.5 * math.log2(math.e)
 STAT_ROWS = 16
 FARTHEST_FIRST = (2, 1, 3, 0)
-NEAREST_FIRST = ((0, 3), (2, 1))
+SECOND_TICK_STEPS = ((2, 1), (3, 0))
 
 
 def frames_stride(count):
@@ -374,10 +374,6 @@
             ),
         )
 
-    for h in range(kv_heads):
-        for copy in cache_copies(h):
-            copy.start()
-
     for copy in late:
         copy.wait()
     frames_copy.wait()
@@ -416,6 +412,10 @@
         def _(k):
             hand_copy(far_first(k)).start()
 
+    for h in range(kv_heads):
+        for copy in cache_copies(h):
+            copy.start()
+
     def incoming(span):
         return jnp.where(
             not_first, handed[:, span].astype(jnp.float32), fresh[:, span].astype(jnp.float32)
@@ -425,7 +425,7 @@
         for copy in cache_arrivals(h):
             copy.wait()
 
-    for steps in NEAREST_FIRST:
+    for steps in SECOND_TICK_STEPS:
 
         @pl.when(not_first)
         def _(steps=steps):

time: 51.2 us -> 49.2 us (0.961)
  the two profiles are of different devices: /device:TPU:3 before, /device:TPU:1 now
where the time goes in v4:
time: 49.2 us; the launch traced here: 49.1 us
  Pallas kernels  48.3 us (98%)
  local copies, waits for them, and re-layouts  0.75 us (2%)
    pallas_call x1, Pallas kernels, attention(): pl.pallas_call(functools.partial(kernel, n_sections, n_chips), out_shape=...  48.3 us

profile of v4, /device:TPU:1, one launch (start us, length us, event | category | flops | bytes accessed | tf_op | source)
XLA Modules:
  0.0 49.1 jit_solution(989796169581403911)
XLA Ops:
  0.0 48.3 %two_ticks.1 = bf16[24,8192]{1,0:T(8,128)(2,1)S(1)} custom-call(bf16[24,8192]{1,0:T(8,128)(2,1)} %bitcast.9, s32[24,64]{1,0:T(8,128)} %bitcast.10, bf16[24,8192]{1,0:T(8,128)(2,1)} %fresh_hbm.1, s32[1,24]{1,0:T(1,128)} %bitcast.11, f32[1,8192]{1,0:T(1,128)} %gain_hbm.1, bf16[768,1024]{1,0:T(8,128)(2,1)} %bitcast.7, bf16[768,1024]{1,0:T(8,128)(2,1)} %bitcast.8, ...), custom_call_target="tpu_custom_call" | custom-call | tf_op jit(solution)/shard_map/two_ticks/pallas_call | solution.py:525
  48.3 0.7 %copy.10 = bf16[1,24,8192]{2,1,0:T(8,128)(2,1)} copy(bf16[1,24,8192]{2,1,0:T(8,128)(2,1)S(1)} %bitcast.6) | data formatting | bytes 786432

commit v5 on v4

--- a/solution.py
+++ b/solution.py
@@ -109,6 +109,20 @@
         step = jnp.where(k % 2 == 1, half - (k + 1) // 2, half + k // 2)
         return (chip + step) % n_chips
 
+    barrier = pltpu.get_barrier_semaphore()
+    for k in range(n_chips - 1):
+        pl.semaphore_signal(barrier, inc=1, device_id=in_line(far_first(k)), device_id_type=MESH)
+
+    @pl.when(not_first)
+    def _():
+        pl.semaphore_signal(barrier, inc=1, device_id=(section - 1, ctx), device_id_type=MESH)
+
+    @pl.when(not_last)
+    def _():
+        pl.semaphore_signal(barrier, inc=1, device_id=(section + 1, ctx), device_id_type=MESH)
+
+    pl.semaphore_signal(barrier, inc=1, device_id=sibling, device_id_type=MESH)
+
     def slot_of(own, h):
         return 2 * h + core if own else 2 * kv_heads + h
 
@@ -141,21 +155,6 @@
     for copy in small:
         copy.start()
 
-    barrier = pltpu.get_barrier_semaphore()
-    pl.semaphore_signal(barrier, inc=1, device_id=sibling, device_id_type=MESH)
-
-    @pl.loop(0, n_chips - 1)
-    def _(k):
-        pl.semaphore_signal(barrier, inc=1, device_id=in_line(far_first(k)), device_id_type=MESH)
-
-    @pl.when(not_first)
-    def _():
-        pl.semaphore_signal(barrier, inc=1, device_id=(section - 1, ctx), device_id_type=MESH)
-
-    @pl.when(not_last)
-    def _():
-        pl.semaphore_signal(barrier, inc=1, device_id=(section + 1, ctx), device_id_type=MESH)
-
     for own in (0, 1):
         for step in FARTHEST_FIRST:
             for copy in loads(own, step):
@@ -231,6 +230,10 @@
     def ship(tick, step, top, totals, weighted):
         h = head_at(step)
         lanes = lax.broadcasted_iota(jnp.int32, (chunk_rows, HD), 1)
+        pick = (
+            lax.broadcasted_iota(jnp.int32, (STAT_ROWS, HD), 0)
+            == lax.broadcasted_iota(jnp.int32, (STAT_ROWS, HD), 1)
+        ).astype(jnp.bfloat16)
         packets = []
         for q in range(chunks_per_head):
             span = slice(q * chunk_rows, (q + 1) * chunk_rows)
@@ -239,9 +242,13 @@
             middle = (stats - high).astype(jnp.bfloat16).astype(jnp.float32)
             low = stats - high - middle
             terms = jnp.where(lanes < 2, high, jnp.where(lanes < 4, middle, low))
+            terms = lax.dot_general(
+                pick, terms.astype(jnp.bfloat16), (((1,), (1,)), ((), ())),
+                preferred_element_type=jnp.float32,
+            )
             terms = jnp.concatenate(
-                [terms, jnp.ones((HD - chunk_rows, HD), jnp.float32)], axis=0
-            ).T[:STAT_ROWS]
+                [terms, jnp.ones((STAT_ROWS, HD - chunk_rows), jnp.float32)], axis=1
+            )
             packets.append(jnp.concatenate([weighted[span], terms], axis=0))
         if step:
             for q in range(chunks_per_head):
@@ -412,20 +419,20 @@
         def _(k):
             hand_copy(far_first(k)).start()
 
-    for h in range(kv_heads):
-        for copy in cache_copies(h):
-            copy.start()
+    for steps in SECOND_TICK_STEPS:
+        for step in steps:
+            for copy in cache_copies(head_at(step)):
+                copy.start()
 
     def incoming(span):
         return jnp.where(
             not_first, handed[:, span].astype(jnp.float32), fresh[:, span].astype(jnp.float32)
         )
 
-    for h in range(kv_heads):
-        for copy in cache_arrivals(h):
-            copy.wait()
-
     for steps in SECOND_TICK_STEPS:
+        for step in steps:
+            for copy in cache_arrivals(head_at(step)):
+                copy.wait()
 
         @pl.when(not_first)
         def _(steps=steps):

time: 49.2 us -> 49.5 us (level)
  the two profiles are of different devices: /device:TPU:1 before, /device:TPU:3 now
where the time goes in v5:
time: 49.5 us; the launch traced here: 49.3 us
  Pallas kernels  48.6 us (98%)
  local copies, waits for them, and re-layouts  0.75 us (2%)
    pallas_call x1, Pallas kernels, attention(): pl.pallas_call(functools.partial(kernel, n_sections, n_chips), out_shape=...  48.6 us

profile of v5, /device:TPU:3, one launch (start us, length us, event | category | flops | bytes accessed | tf_op | source)
XLA Modules:
  0.0 49.3 jit_solution(1921042711179575472)
XLA Ops:
  0.0 48.6 %two_ticks.1 = bf16[24,8192]{1,0:T(8,128)(2,1)S(1)} custom-call(bf16[24,8192]{1,0:T(8,128)(2,1)} %bitcast.9, s32[24,64]{1,0:T(8,128)} %bitcast.10, bf16[24,8192]{1,0:T(8,128)(2,1)} %fresh_hbm.1, s32[1,24]{1,0:T(1,128)} %bitcast.11, f32[1,8192]{1,0:T(1,128)} %gain_hbm.1, bf16[768,1024]{1,0:T(8,128)(2,1)} %bitcast.7, bf16[768,1024]{1,0:T(8,128)(2,1)} %bitcast.8, ...), custom_call_target="tpu_custom_call" | custom-call | tf_op jit(solution)/shard_map/two_ticks/pallas_call | solution.py:532
  48.6 0.7 %copy.10 = bf16[1,24,8192]{2,1,0:T(8,128)(2,1)} copy(bf16[1,24,8192]{2,1,0:T(8,128)(2,1)S(1)} %bitcast.6) | data formatting | bytes 786432

commit v6 on v4

--- a/solution.py
+++ b/solution.py
@@ -412,20 +412,20 @@
         def _(k):
             hand_copy(far_first(k)).start()
 
-    for h in range(kv_heads):
-        for copy in cache_copies(h):
-            copy.start()
+    for steps in SECOND_TICK_STEPS:
+        for step in steps:
+            for copy in cache_copies(head_at(step)):
+                copy.start()
 
     def incoming(span):
         return jnp.where(
             not_first, handed[:, span].astype(jnp.float32), fresh[:, span].astype(jnp.float32)
         )
 
-    for h in range(kv_heads):
-        for copy in cache_arrivals(h):
-            copy.wait()
-
     for steps in SECOND_TICK_STEPS:
+        for step in steps:
+            for copy in cache_arrivals(head_at(step)):
+                copy.wait()
 
         @pl.when(not_first)
         def _(steps=steps):

time: 49.2 us -> 49.2 us (level)
  the two profiles are of different devices: /device:TPU:1 before, /device:TPU:3 now
where the time goes in v6:
time: 49.2 us; the launch traced here: 49 us
  Pallas kernels  48.3 us (98%)
  local copies, waits for them, and re-layouts  0.75 us (2%)
    pallas_call x1, Pallas kernels, attention(): pl.pallas_call(functools.partial(kernel, n_sections, n_chips), out_shape=...  48.3 us

profile of v6, /device:TPU:3, one launch (start us, length us, event | category | flops | bytes accessed | tf_op | source)
XLA Modules:
  0.0 49.0 jit_solution(2569382008094461841)
XLA Ops:
  0.0 48.3 %two_ticks.1 = bf16[24,8192]{1,0:T(8,128)(2,1)S(1)} custom-call(bf16[24,8192]{1,0:T(8,128)(2,1)} %bitcast.9, s32[24,64]{1,0:T(8,128)} %bitcast.10, bf16[24,8192]{1,0:T(8,128)(2,1)} %fresh_hbm.1, s32[1,24]{1,0:T(1,128)} %bitcast.11, f32[1,8192]{1,0:T(1,128)} %gain_hbm.1, bf16[768,1024]{1,0:T(8,128)(2,1)} %bitcast.7, bf16[768,1024]{1,0:T(8,128)(2,1)} %bitcast.8, ...), custom_call_target="tpu_custom_call" | custom-call | tf_op jit(solution)/shard_map/two_ticks/pallas_call | solution.py:525
  48.3 0.7 %copy.10 = bf16[1,24,8192]{2,1,0:T(8,128)(2,1)} copy(bf16[1,24,8192]{2,1,0:T(8,128)(2,1)S(1)} %bitcast.6) | data formatting | bytes 786432
